TPU v7x, 32 devices: a whole 2x2x4 slice. The times are simulated.
32 devices in a mesh: center: 8 (over z, y), rep: 4 (over x, core).
Axes of the slice: x: 2, y: 2, z: 4, core: 2. Of those that a mesh axis runs over, the one named last changes fastest.
Arguments:
- faces: bfloat16 [2048, 512], P(('center', 'rep')), may hold values from -1800 to 1800
- w_first: bfloat16 [512, 512], replicated, may hold values from -1.1 to 1.1
- w_second: bfloat16 [512, 512], replicated, may hold values from -1.1 to 1.1
- gain_first: float32 [512], replicated, may hold values from 0.46 to 1.54
- bias_first: float32 [512], replicated, may hold values from -3 to 3
- gain_second: float32 [512], replicated, may hold values from 0.46 to 1.54
- centers: float32 [16384, 512], P('center'), may hold values from -6 to 6
- momentum: float32 [16384, 512], P('center'), may hold values from -1.2 to 1.2
- sample_index: int32 [1024], P('center'), may hold values from 0 to 2047, as said below
- live_count: int32 [8], P('center'), may hold values from 16 to 128, as said below
- labels: int32 [2048], P(('center', 'rep')), may hold values from 0 to 1023, as said below
Outputs:
- loss: float32 [2048], P(('center', 'rep'))
- feat_grad: float32 [2048, 512], P(('center', 'rep'))
- new_centers: float32 [1024, 512], P('center')
- new_momentum: float32 [1024, 512], P('center')
Inputs may be any that keep to these rules, and one draw needn't show every extreme that they name: `sample_index`: the 128 entries of one shard are distinct rows of that shard. The live slots of a shard are its first live_count entries; some shard has 128 of them and some shard 128 // 8. `labels`: each label is a live sampled slot, counted over all shards' lists in shard order.
All inputs are finite; a program needn't handle non-finite values.
Results may differ from a plain program's by a relative error of at most 0.0075.
Values may be sent and summed in bfloat16 or wider, within the bound.
No kernel may reach another device: no remote copies, remote signals or barrier semaphores. Data moves between devices by JAX's collectives and lax.ppermute only.
A program may use at most 64 MiB of HBM per device.

v0:
```python
import jax
import jax.numpy as jnp
from jax import lax
from jax.sharding import PartitionSpec as P

LOGIT_SCALE = 64.0
COS_MARGIN = 0.35
LEARN_RATE = 0.5
MOMENT_COEF = 0.9
DECAY_COEF = 0.0005
NORM_EPS = 1e-05
LENGTH_EPS = 1e-06


def batch_norm(values, gain_vec, sample_count):
    summed, squares = lax.psum((jnp.sum(values, 0), jnp.sum(values * values, 0)), "rep")
    mean_vec = summed / sample_count
    spread = squares / sample_count - mean_vec * mean_vec
    return gain_vec * (values - mean_vec) * lax.rsqrt(spread + NORM_EPS)


def momentum_step(raw_grad, picked, center_len, center_unit, picked_momentum, live_slot):
    center_radial = jnp.sum(center_unit * raw_grad, 1, keepdims=True)
    center_grad = (raw_grad - center_unit * center_radial) / center_len
    velocity = MOMENT_COEF * picked_momentum + center_grad + DECAY_COEF * picked
    velocity = jnp.where(live_slot[:, None], velocity, picked_momentum)
    placed = jnp.where(live_slot[:, None], picked - LEARN_RATE * velocity, picked)
    return (placed, velocity)


def per_device(
    faces,
    w_first,
    w_second,
    gain_first,
    bias_first,
    gain_second,
    centers,
    momentum,
    sample_index,
    live_count,
    labels,
):
    face_rows = faces.shape[0]
    width = faces.shape[1]
    sample_count = face_rows * lax.axis_size("rep")
    first_out = jnp.dot(faces, w_first, preferred_element_type=jnp.float32)
    hidden = jnp.maximum(batch_norm(first_out, gain_first, sample_count) + bias_first, 0.0).astype(
        jnp.bfloat16
    )
    second = jnp.dot(hidden, w_second, preferred_element_type=jnp.float32)
    feature = batch_norm(second, gain_second, sample_count)
    length = jnp.sqrt(jnp.sum(feature * feature, 1, keepdims=True) + LENGTH_EPS)
    unit_rows = feature / length
    unit_low = unit_rows.astype(jnp.bfloat16)
    all_units, all_labels = (
        lax.all_gather(unit_low, "center", axis=0, tiled=True),
        lax.all_gather(labels, "center", axis=0, tiled=True),
    )
    my_shard = lax.axis_index("center")
    picked = jnp.take(centers, sample_index, axis=0)
    picked_momentum = jnp.take(momentum, sample_index, axis=0)
    center_len = jnp.sqrt(jnp.sum(picked * picked, 1, keepdims=True) + LENGTH_EPS)
    center_unit = picked / center_len
    center_low = center_unit.astype(jnp.bfloat16)
    slot_count = picked.shape[0]
    slot_ids = jnp.arange(slot_count, dtype=jnp.int32)
    live_slot = slot_ids < live_count[0]
    first_slot = my_shard * slot_count
    group_rows = all_units.shape[0]
    block_rows = min(1024, group_rows)
    block_total_count = group_rows // block_rows
    unit_blocks = all_units.reshape(block_total_count, block_rows, width)
    mark_blocks = all_labels.reshape(block_total_count, block_rows)

    def target_of(mark_block):
        return (mark_block - first_slot)[:, None] == slot_ids[None, :]

    def partials(element):
        cosine = jnp.einsum("fd,sd->fs", element[0], center_low, preferred_element_type=jnp.float32)
        target = target_of(element[1])
        logits = LOGIT_SCALE * (cosine - COS_MARGIN * target.astype(jnp.float32))
        exponent = jnp.where(live_slot[None, :], jnp.exp(logits), 0.0)
        return (exponent, jnp.sum(exponent, 1), jnp.sum(jnp.where(target, logits, 0.0), 1))

    exponent_blocks, local_total, local_target = lax.map(partials, (unit_blocks, mark_blocks))
    softmax_total, target_logit = lax.psum(
        (local_total.reshape(group_rows), local_target.reshape(group_rows)), "center"
    )
    group_loss = jnp.log(softmax_total) - target_logit
    loss = lax.dynamic_slice_in_dim(group_loss, my_shard * face_rows, face_rows, 0)
    total_blocks = softmax_total.reshape(block_total_count, block_rows)

    def grad_weight(exponent, mark_block, block_total):
        target = target_of(mark_block)
        return (
            LOGIT_SCALE * (exponent / block_total[:, None] - target.astype(jnp.float32))
        ).astype(jnp.bfloat16)

    start_sum = jnp.zeros((slot_count, width), jnp.float32)

    def both_block(running, element):
        weight = grad_weight(element[2], element[1], element[3])
        running = running + jnp.einsum(
            "fs,fd->sd", weight, element[0], preferred_element_type=jnp.float32
        )
        return (running, jnp.dot(weight, center_low, preferred_element_type=jnp.float32))

    center_raw, unit_terms = lax.scan(
        both_block, start_sum, (unit_blocks, mark_blocks, exponent_blocks, total_blocks)
    )
    unit_grad = lax.psum_scatter(
        unit_terms.reshape(group_rows, width), "center", scatter_dimension=0, tiled=True
    )
    radial = jnp.sum(unit_rows * unit_grad, 1, keepdims=True)
    feat_grad = (unit_grad - unit_rows * radial) / length
    raw_grad = lax.psum(center_raw, "rep")
    new_centers, new_momentum = momentum_step(
        raw_grad, picked, center_len, center_unit, picked_momentum, live_slot
    )
    return (loss, feat_grad, new_centers, new_momentum)


def solution(mesh):
    return jax.shard_map(
        per_device,
        mesh=mesh,
        in_specs=(
            P(("center", "rep"), None),
            P(),
            P(),
            P(),
            P(),
            P(),
            P("center", None),
            P("center", None),
            P("center"),
            P("center"),
            P(("center", "rep")),
        ),
        out_specs=(
            P(("center", "rep")),
            P(("center", "rep"), None),
            P("center", None),
            P("center", None),
        ),
        check_vma=False,
    )
```

profile of v0, /device:TPU:0, one launch (start us, length us, event | category | flops | bytes accessed | tf_op | source)
XLA Modules:
  0.0 172.2 jit_solution(15847876268697771019)
XLA Ops:
  8.8 0.7 compare_select_fusion
  9.4 0.7 compare_and_fusion
  10.1 1.2 dynamic-slice.4
  12.0 0.9 dynamic-update-slice
  12.8 13.1 %all-reduce = s32[512]{0:T(512)S(1)} all-reduce(s32[512]{0:T(512)S(1)} %dynamic-update-slice), channel_id=1, replica_groups=mesh['center'=8,'rep'=4] {'center'}, use_global_device_ids=true, to_apply=%add | all-reduce | flops 512 | bytes 4096
  25.9 1.1 fusion.16
  27.0 5.7 %all-reduce.3 = (f32[512]{0:T(512)S(1)}, f32[512]{0:T(512)S(1)}) all-reduce(f32[512]{0:T(512)S(1)} %get-tuple-element.60, f32[512]{0:T(512)S(1)} %get-tuple-element.49), channel_id=1, replica_groups=mesh['center'=8,'rep'=4] {'rep'}, use_global_device_ids=true, to_apply=%region_3.0 | all-reduce | flops 1024 | bytes 8192 | tf_op jit(solution)/shard_map/psum | solution.py:16
  32.7 1.3 fusion.15
  34.0 6.6 %all-reduce.2 = (f32[512]{0:T(512)S(1)}, f32[512]{0:T(512)S(1)}) all-reduce(f32[512]{0:T(512)S(1)} %get-tuple-element.48, f32[512]{0:T(512)S(1)} %get-tuple-element.47), channel_id=1, replica_groups=mesh['center'=8,'rep'=4] {'rep'}, use_global_device_ids=true, to_apply=%region_7.0 | all-reduce | flops 1024 | bytes 8192 | tf_op jit(solution)/shard_map/psum | solution.py:16
  40.6 0.8 multiply_reduce_fusion.3
  41.5 0.8 fusion.13
  42.2 3.1 %gather_fusion = f32[128,512]{1,0:T(8,128)S(1)} fusion(f32[2048,512]{1,0:T(8,128)} %param.19, s32[1024]{0:T(1024)S(1)} %pad_clamp_fusion), kind=kCustom, calls=%fused_computation.clone | custom fusion | bytes 524800 | tf_op jit(solution)/shard_map/jit(_take)/gather | solution.py:61
  45.5 31.2 %all_gather.6 = bf16[512,512]{1,0:T(8,128)(2,1)S(1)} all-gather(bf16[64,512]{1,0:T(8,128)(2,1)S(1)} %fusion.13), channel_id=1, replica_groups=mesh['center'=8,'rep'=4] {'center'}, dimensions={0}, use_global_device_ids=true | all-gather | bytes 589824 | tf_op jit(solution)/shard_map/all_gather | solution.py:57
  77.1 18.9 %all-reduce.1 = (f32[512]{0:T(512)S(1)}, f32[512]{0:T(512)S(1)}) all-reduce(f32[512]{0:T(512)S(1)} %get-tuple-element.46, f32[512]{0:T(512)S(1)} %get-tuple-element.45), channel_id=1, replica_groups=mesh['center'=8,'rep'=4] {'center'}, use_global_device_ids=true, to_apply=%region_13.15 | all-reduce | flops 1024 | bytes 8192 | tf_op jit(solution)/shard_map/psum | solution.py:87
  96.0 1.0 fusion.14
  97.1 1.4 fusion.4
  98.5 3.1 %gather_fusion.1 = f32[128,512]{1,0:T(8,128)S(1)} fusion(f32[2048,512]{1,0:T(8,128)} %param.20, s32[1024]{0:T(1024)S(1)} %pad_clamp_fusion), kind=kCustom, calls=%fused_computation.1.clone | custom fusion | bytes 524800 | tf_op jit(solution)/shard_map/jit(_take)/gather | solution.py:62
  101.6 0.6 dynamic_slice.19
  102.2 23.7 %all-reduce.6.cloned.1.call-done = f32[128,512]{1,0:T(8,128)} async-done(((f32[128,512]{1,0:T(8,128)}), f32[128,512]{1,0:T(8,128)}) %all-reduce.6.cloned.1.call-update) | async-done | bytes 262160 | tf_op jit(solution)/shard_map/psum | solution.py:117
  126.0 1.1 multiply_reduce_fusion
  127.1 1.9 %subtract_select_fusion = (f32[128,512]{1,0:T(8,128)}, f32[128,512]{1,0:T(8,128)}) fusion(f32[128,512]{1,0:T(8,128)S(1)} %gather_fusion, pred[128]{0:T(512)(128)(4,1)S(1)} %get-tuple-element.86, pred[128]{0:T(512)(128)(4,1)S(1)} %get-tuple-element.87, f32[128,512]{1,0:T(8,128)} %all-reduce.6.cloned.1.call-done, f32[128]{0:T(128)S(1)} %multiply_reduce_fusion, ...), kind=kLoop, calls=%fused_computation.4 | loop fusion | flops 917504 | bytes 1312000 | tf_op jit(solution)/shard_map/jit(_where)/select_n | solution.py:27
  129.1 33.0 %reduce-scatter.2.cloned.1.call-done = f32[64,512]{1,0:T(8,128)} async-done(((f32[512,512]{1,0:T(8,128)}), f32[64,512]{1,0:T(8,128)}) %reduce-scatter.2.cloned.1.call-update) | async-done | bytes 131088 | tf_op jit(solution)/shard_map/reduce_scatter | solution.py:112
  162.0 1.1 multiply_reduce_fusion.2
  163.1 1.7 subtract_divide_fusion
  (18 shorter events, 0.7 us)
Async XLA Ops:
  8.0 17.9 %copy-start = (bf16[512,512]{1,0:T(8,128)(2,1)S(1)}, bf16[512,512]{1,0:T(8,128)(2,1)}, u32[]{:S(2)}) copy-start(bf16[512,512]{1,0:T(8,128)(2,1)} %param.14) | copy-start | bytes 1572868
  8.0 118.0 %all-reduce.6.cloned.1.call-start = ((), (), s32[]{:S(2)}) async-start(), calls=%async_computation.2 | async-start | bytes 524288 | tf_op jit(solution)/shard_map/psum | solution.py:117
  97.0 65.0 %copy-start.1 = (f32[512]{0:T(512)S(1)}, f32[512]{0:T(512)}, u32[]{:S(2)}) copy-start(f32[512]{0:T(512)} %param.18) | copy-start | bytes 6148
  97.1 65.0 %reduce-scatter.2.cloned.1.call-start = ((), (), s32[]{:S(2)}) async-start(), calls=%async_computation.1 | async-start | bytes 1179648 | tf_op jit(solution)/shard_map/reduce_scatter | solution.py:112
Sparse Core Ops, SparseCore 0:
  97.2 28.7 all-reduce.5
Sparse Core Ops, SparseCore 1:
  100.9 61.0 reduce-scatter.1
where the time goes:
time: 173 us; the launch traced here: 172 us
  blocking collectives  75.5 us (44%)
  waiting for transfers between devices  56.7 us (33%)
  between operations  16.9 us (10%)
  other arithmetic  8.98 us (5%)
  local copies, waits for them, and re-layouts  8.84 us (5%)
  matrix products  5.14 us (3%)
    reduce_scatter x1, waiting for transfers between devices, per_device(): lax.psum_scatter(unit_terms.reshape(group_rows, width), 'center', scatter...  33 us
    all_gather x1, blocking collectives, per_device(): lax.all_gather(unit_low, 'center', axis=0, tiled=True)  31.2 us
    psum x1, waiting for transfers between devices, per_device(): raw_grad = lax.psum(center_raw, 'rep')  23.7 us
    psum x1, blocking collectives, per_device(): lax.psum((local_total.reshape(group_rows), local_target.reshape(group_row...  18.9 us
    unnamed x1, blocking collectives  13.1 us
    psum x2, blocking collectives, batch_norm(): lax.psum((jnp.sum(values, 0), jnp.sum(values * values, 0)), 'rep')  12.3 us
  transfers between devices with their start and end apart: 2, of which 2 were waited for; matrix products, arithmetic and copies ran while one was open for 5% of the time, Pallas kernels for 0%

commit v1 on v0

v1 whole, which is shorter than its diff:
```python
import functools

import jax
import jax.numpy as jnp
from jax import lax
from jax.experimental import pallas as pl
from jax.experimental.pallas import tpu as pltpu
from jax.sharding import PartitionSpec as P


LOGIT_SCALE = 64.0
COS_MARGIN = 0.35
LEARN_RATE = 0.5
MOMENT_COEF = 0.9
DECAY_COEF = 0.0005
NORM_EPS = 1e-05
LENGTH_EPS = 1e-06
DEAD_MARK = 2.0
LABEL_BASE = 128
LABEL_ROWS = 16

F32 = jnp.float32
BF16 = jnp.bfloat16
VMEM = pl.BlockSpec(memory_space=pltpu.VMEM)
HBM = pl.BlockSpec(memory_space=pltpu.HBM)
SMEM = pl.BlockSpec(memory_space=pltpu.SMEM)
PARAMS = pltpu.CompilerParams(vmem_limit_bytes=16 * 2**20)


def swap(value, axis, mask):
    size = lax.axis_size(axis)
    return lax.ppermute(value, axis, [(i, i ^ mask) for i in range(size)])


def rep_bits():
    bit = lax.axis_size("rep") >> 1
    while bit:
        yield bit
        bit >>= 1


def stages_of(size):
    bits = size.bit_length() - 1
    stages, low = [], 0
    while low < bits:
        take = 1 if low == 0 else min(2, bits - low)
        stages.append([step << low for step in range(1, 1 << take)])
        low += take
    return stages


def spread_rep(value):
    reps = lax.axis_size("rep")
    masks = [0]
    for bit in rep_bits():
        value = jnp.concatenate([value, swap(value, "rep", bit)], axis=0)
        masks += [mask | bit for mask in masks]
    assert len(masks) == reps
    return value, masks


def entry_kernel(index_ref, live_ref, centers_ref, faces_ref, labels_ref, low_ref, pack_ref, line_ref, index, labels, rows_ref, sems):
    quarter, width = low_ref.shape
    face_rows = faces_ref.shape[0]
    first = lax.axis_index("rep") * quarter
    index_copy = pltpu.make_async_copy(index_ref, index, sems.at[0])
    faces_copy = pltpu.make_async_copy(faces_ref, pack_ref.at[pl.ds(0, face_rows)], sems.at[2])
    labels_copy = pltpu.make_async_copy(labels_ref, labels, sems.at[3])
    index_copy.start()
    labels_copy.start()
    faces_copy.start()
    index_copy.wait()
    for i in range(quarter):
        row = index[first + i]
        pltpu.make_async_copy(centers_ref.at[pl.ds(row, 1)], rows_ref.at[pl.ds(i, 1)], sems.at[4]).start()
    labels_copy.wait()
    marks = jnp.concatenate([labels[...]] * (width // face_rows), axis=1)
    line = lax.broadcasted_iota(jnp.int32, (LABEL_ROWS, width), 0)
    digits = jnp.where(line == 0, marks // LABEL_BASE, jnp.where(line == 1, marks % LABEL_BASE, 0))
    pack_ref[face_rows:] = digits.astype(F32).astype(BF16)
    line_ref[...] = jnp.full(line_ref.shape, live_ref[0], jnp.int32)
    faces_copy.wait()
    pltpu.make_async_copy(rows_ref, rows_ref, sems.at[4]).wait()
    picked = rows_ref[...]
    unit = picked / jnp.sqrt(jnp.sum(picked * picked, 1, keepdims=True) + LENGTH_EPS)
    slot = lax.broadcasted_iota(jnp.int32, (quarter, width), 0) + first
    low_ref[...] = jnp.where(slot < live_ref[0], unit, DEAD_MARK).astype(BF16)


def rows_kernel(index_ref, centers_ref, momentum_ref, after_ref, picked_ref, moment_ref, index, sems):
    del after_ref
    index_copy = pltpu.make_async_copy(index_ref, index, sems.at[2])
    index_copy.start()
    index_copy.wait()
    for i in range(index.shape[0]):
        row = index[i]
        pltpu.make_async_copy(centers_ref.at[pl.ds(row, 1)], picked_ref.at[pl.ds(i, 1)], sems.at[0]).start()
        pltpu.make_async_copy(momentum_ref.at[pl.ds(row, 1)], moment_ref.at[pl.ds(i, 1)], sems.at[1]).start()
    pltpu.make_async_copy(picked_ref, picked_ref, sems.at[0]).wait()
    pltpu.make_async_copy(moment_ref, moment_ref, sems.at[1]).wait()


def normalized(values, gain):
    count = values.shape[0]
    centered = values - jnp.sum(values, 0, keepdims=True) / count
    spread = jnp.sum(centered * centered, 0, keepdims=True) / count
    return centered * (gain * lax.rsqrt(spread + NORM_EPS))


def head_kernel(
    w_first_ref, w_second_ref, gain_first_ref, bias_first_ref, gain_second_ref, packs_ref, low_ref, feature_ref, label_ref, w_first, w_second, sems
):
    first_copy = pltpu.make_async_copy(w_first_ref, w_first, sems.at[0])
    second_copy = pltpu.make_async_copy(w_second_ref, w_second, sems.at[1])
    first_copy.start()
    second_copy.start()
    face_rows = feature_ref.shape[0]
    each = face_rows + LABEL_ROWS
    packs = [packs_ref[at * each : (at + 1) * each] for at in range(packs_ref.shape[0] // each)]
    faces = jnp.concatenate([pack[:face_rows] for pack in packs], axis=0)
    group = label_ref.shape[1]
    part = lax.broadcasted_iota(jnp.int32, (LABEL_ROWS, group), 1) // face_rows
    digits = packs[0][face_rows:, :group].astype(F32)
    for at, pack in enumerate(packs[1:], 1):
        digits = jnp.where(part == at, pack[face_rows:, :group].astype(F32), digits)
    label_ref[...] = jnp.broadcast_to(digits[0:1] * LABEL_BASE + digits[1:2], label_ref.shape).astype(jnp.int32)
    first_copy.wait()
    first = jnp.dot(faces, w_first[...], preferred_element_type=F32)
    hidden = jnp.maximum(normalized(first, gain_first_ref[...]) + bias_first_ref[...], 0.0).astype(BF16)
    second_copy.wait()
    second = jnp.dot(hidden, w_second[...], preferred_element_type=F32)
    feature = normalized(second, gain_second_ref[...])
    length = jnp.sqrt(jnp.sum(feature * feature, 1, keepdims=True) + LENGTH_EPS)
    low_ref[...] = (feature / length).astype(BF16)
    feature_ref[...] = feature[:face_rows]


def target_of(label_ref, slots, quarter, slot_count):
    at = lax.broadcasted_iota(jnp.int32, (slots, label_ref.shape[1]), 0)
    shard = lax.axis_index("center") ^ (at // quarter)
    slot = shard * slot_count + lax.axis_index("rep") * quarter + at % quarter
    return slot == label_ref[0:1]


def score_kernel(quarter, slot_count, unit_ref, label_ref, *refs):
    blocks, (exponent_ref, sums_ref) = refs[:-2], refs[-2:]
    rows = jnp.concatenate([block[...] for block in blocks], axis=0)
    cosine = lax.dot_general(rows, unit_ref[...], (((1,), (1,)), ((), ())), preferred_element_type=F32)
    target = target_of(label_ref, rows.shape[0], quarter, slot_count)
    logits = LOGIT_SCALE * (cosine - jnp.where(target, COS_MARGIN, 0.0))
    live = rows[:, 0:1].astype(F32) < DEAD_MARK
    exponent = jnp.where(live, jnp.exp(logits), 0.0)
    exponent_ref[...] = exponent
    total = jnp.sum(exponent, 0, keepdims=True)
    own = jnp.sum(jnp.where(target, logits, 0.0), 0, keepdims=True)
    line = lax.broadcasted_iota(jnp.int32, sums_ref.shape, 0)
    sums_ref[...] = jnp.where(line == 0, total, own)


def fold_lanes(sums, bit, face_rows):
    count = sums.shape[1] // face_rows
    parts = [sums[:, (at ^ bit) * face_rows : ((at ^ bit) + 1) * face_rows] for at in range(count)]
    return jnp.concatenate(parts, axis=1)


def total_kernel(bit, face_rows, own_ref, other_ref, out_ref):
    out_ref[...] = own_ref[...] + fold_lanes(other_ref[...], bit, face_rows)


def grad_kernel(quarter, slot_count, unit_ref, label_ref, exponent_ref, own_ref, other_ref, *refs):
    blocks, (loss_ref, kept_ref, face_ref, even_ref, odd_ref) = refs[:-5], refs[-5:]
    group = unit_ref.shape[0]
    face_rows = loss_ref.shape[1]
    summed = own_ref[...] + fold_lanes(other_ref[...], 1, face_rows)
    total = summed[0:1]
    loss_ref[...] = (jnp.log(total) - summed[1:2])[:, :face_rows]
    rows = jnp.concatenate([block[...] for block in blocks], axis=0)
    target = target_of(label_ref, rows.shape[0], quarter, slot_count)
    share = exponent_ref[...] / total
    weight = (LOGIT_SCALE * (share - jnp.where(target, 1.0, 0.0))).astype(BF16)
    raw = jnp.dot(weight, unit_ref[...], preferred_element_type=F32)
    for at in range(rows.shape[0] // quarter):
        half = odd_ref if at % 2 else even_ref
        half[pl.ds(at // 2 * quarter, quarter)] = raw[at * quarter : (at + 1) * quarter].astype(half.dtype)
    unit_grad = lax.dot_general(weight, rows, (((0,), (0,)), ((), ())), preferred_element_type=F32)
    kept_ref[...] = unit_grad[: group // 2]
    face_ref[...] = unit_grad[group // 2 :].astype(BF16)


def fold_kernel(parts, kept_ref, *refs):
    takes, (own_ref, *outs) = refs[:parts], refs[parts:]
    summed = kept_ref[...]
    for item in takes:
        summed = summed + item[...].astype(F32)
    rows = own_ref.shape[0]
    own_ref[...] = summed[:rows].astype(own_ref.dtype)
    for at, out in enumerate(outs, 1):
        out[...] = summed[at * rows : (at + 1) * rows].astype(BF16)


def half_kernel(kept_ref, received_ref, own_ref, sent_ref):
    rows = own_ref.shape[0]
    summed = kept_ref[...] + received_ref[...].astype(F32)
    own_ref[...] = summed[:rows]
    sent_ref[...] = summed[rows:].astype(BF16)


def face_kernel(feature_ref, own_ref, received_ref, grad_ref):
    feature = feature_ref[...]
    length = jnp.sqrt(jnp.sum(feature * feature, 1, keepdims=True) + LENGTH_EPS)
    unit = feature / length
    unit_grad = own_ref[...] + received_ref[...].astype(F32)
    radial = jnp.sum(unit * unit_grad, 1, keepdims=True)
    grad_ref[...] = (unit_grad - unit * radial) / length


def step_kernel(masks, live_ref, picked_ref, moment_ref, raws_ref, placed_ref, velocity_ref, raw_ref):
    quarter = raws_ref.shape[0] // len(masks)
    rep = lax.axis_index("rep")
    for at, mask in enumerate(masks):
        item = raws_ref[at * quarter : (at + 1) * quarter].astype(F32)
        raw_ref[pl.ds(pl.multiple_of((rep ^ mask) * quarter, quarter), quarter)] = item
    raw = raw_ref[...]
    picked = picked_ref[...]
    moment = moment_ref[...]
    length = jnp.sqrt(jnp.sum(picked * picked, 1, keepdims=True) + LENGTH_EPS)
    unit = picked / length
    radial = jnp.sum(unit * raw, 1, keepdims=True)
    grad = (raw - unit * radial) / length
    live = lax.broadcasted_iota(jnp.int32, picked.shape, 0) < live_ref[0:1, 0:1]
    velocity = jnp.where(live, MOMENT_COEF * moment + grad + DECAY_COEF * picked, moment)
    velocity_ref[...] = velocity
    placed_ref[...] = jnp.where(live, picked - LEARN_RATE * velocity, picked)


def per_device(
    faces,
    w_first,
    w_second,
    gain_first,
    bias_first,
    gain_second,
    centers,
    momentum,
    sample_index,
    live_count,
    labels,
):
    face_rows, width = faces.shape
    faces, w_first, w_second, centers, momentum, sample_index, labels = (
        pltpu.with_memory_space_constraint(value, pltpu.HBM)
        for value in (faces, w_first, w_second, centers, momentum, sample_index, labels.reshape(1, face_rows))
    )
    reps = lax.axis_size("rep")
    shards = lax.axis_size("center")
    slot_count = sample_index.shape[0]
    quarter = slot_count // reps
    group = face_rows * reps
    slots = quarter * shards
    shape = jax.ShapeDtypeStruct

    low, pack, live_line = pl.pallas_call(
        entry_kernel,
        in_specs=[HBM, SMEM, HBM, HBM, HBM],
        out_specs=[VMEM] * 3,
        out_shape=[
            shape((quarter, width), BF16),
            shape((face_rows + LABEL_ROWS, width), BF16),
            shape((8, 128), jnp.int32),
        ],
        scratch_shapes=[
            pltpu.SMEM((slot_count,), jnp.int32),
            pltpu.VMEM((1, face_rows), jnp.int32),
            pltpu.VMEM((quarter, width), F32),
            pltpu.SemaphoreType.DMA((5,)),
        ],
        compiler_params=PARAMS,
        name="entry",
    )(sample_index, live_count, centers, faces, labels)

    blocks = [low]
    stages = stages_of(shards)
    for masks in stages:
        joined = jnp.concatenate(blocks, axis=0) if len(blocks) > 1 else blocks[0]
        blocks = [joined] + [swap(joined, "center", mask) for mask in masks]

    packs, masks = spread_rep(pack)
    order = [masks.index(at) for at in range(reps)]
    each = face_rows + LABEL_ROWS
    if order != list(range(reps)):
        packs = jnp.concatenate([packs[at * each : (at + 1) * each] for at in order], axis=0)
    unit_low, feature, label_line = pl.pallas_call(
        head_kernel,
        in_specs=[HBM] * 2 + [VMEM] * 4,
        out_specs=[VMEM] * 3,
        out_shape=[shape((group, width), BF16), shape((face_rows, width), F32), shape((8, group), jnp.int32)],
        scratch_shapes=[pltpu.VMEM((width, width), BF16)] * 2 + [pltpu.SemaphoreType.DMA((2,))],
        compiler_params=PARAMS,
        name="head",
    )(w_first, w_second, gain_first.reshape(1, width), bias_first.reshape(1, width), gain_second.reshape(1, width), packs)

    exponent, sums = pl.pallas_call(
        functools.partial(score_kernel, quarter, slot_count),
        in_specs=[VMEM] * (2 + len(blocks)),
        out_specs=[VMEM] * 2,
        out_shape=[shape((slots, group), F32), shape((8, group), F32)],
        compiler_params=PARAMS,
        name="score",
    )(unit_low, label_line, *blocks)

    bits = list(rep_bits())
    for bit in bits[:-1]:
        sums = pl.pallas_call(
            functools.partial(total_kernel, bit, face_rows),
            in_specs=[VMEM] * 2,
            out_specs=VMEM,
            out_shape=shape((8, group), F32),
            compiler_params=PARAMS,
            name="total",
        )(sums, swap(sums, "rep", bit))
    loss, face_kept, face_sent, kept, sent = pl.pallas_call(
        functools.partial(grad_kernel, quarter, slot_count),
        in_specs=[VMEM] * (5 + len(blocks)),
        out_specs=[VMEM] * 5,
        out_shape=[
            shape((1, face_rows), F32),
            shape((group // 2, width), F32),
            shape((group // 2, width), BF16),
            shape((slots // 2, width), F32),
            shape((slots // 2, width), BF16),
        ],
        compiler_params=PARAMS,
        name="grad",
    )(unit_low, label_line, exponent, sums, swap(sums, "rep", 1), *blocks)

    picked, moment = pl.pallas_call(
        rows_kernel,
        in_specs=[HBM] * 3 + [VMEM],
        out_specs=[VMEM, VMEM],
        out_shape=[shape((slot_count, width), F32)] * 2,
        scratch_shapes=[pltpu.SMEM((slot_count,), jnp.int32), pltpu.SemaphoreType.DMA((3,))],
        compiler_params=PARAMS,
        name="rows",
    )(sample_index, centers, momentum, loss)

    received = [swap(sent, "center", 1)]
    for later in stages[:0:-1] + [[]]:
        rows = kept.shape[0] // (len(later) + 1)
        kept, *sends = pl.pallas_call(
            functools.partial(fold_kernel, len(received)),
            in_specs=[VMEM] * (1 + len(received)),
            out_specs=[VMEM] * (1 + len(later)),
            out_shape=[shape((rows, width), F32 if later else BF16)] + [shape((rows, width), BF16)] * len(later),
            compiler_params=PARAMS,
            name="fold",
        )(kept, *received)
        received = [swap(item, "center", mask) for mask, item in zip(later, sends)]

    for bit in bits[:-1]:
        half = face_kept.shape[0] // 2
        face_kept, face_sent = pl.pallas_call(
            half_kernel,
            in_specs=[VMEM] * 2,
            out_specs=[VMEM] * 2,
            out_shape=[shape((half, width), F32), shape((half, width), BF16)],
            compiler_params=PARAMS,
            name="half",
        )(face_kept, swap(face_sent, "rep", bit))
    feat_grad = pl.pallas_call(
        face_kernel,
        in_specs=[VMEM] * 3,
        out_specs=VMEM,
        out_shape=shape((face_rows, width), F32),
        compiler_params=PARAMS,
        name="face",
    )(feature, face_kept, swap(face_sent, "rep", bits[-1]))

    raws, masks = spread_rep(kept)
    new_centers, new_momentum = pl.pallas_call(
        functools.partial(step_kernel, masks),
        in_specs=[VMEM] * 4,
        out_specs=[VMEM] * 2,
        out_shape=[shape((slot_count, width), F32)] * 2,
        scratch_shapes=[pltpu.VMEM((slot_count, width), F32)],
        compiler_params=PARAMS,
        name="step",
    )(live_line, picked, moment, raws)
    return (loss.reshape(face_rows), feat_grad, new_centers, new_momentum)


def solution(mesh):
    return jax.shard_map(
        per_device,
        mesh=mesh,
        in_specs=(
            P(("center", "rep"), None),
            P(),
            P(),
            P(),
            P(),
            P(),
            P("center", None),
            P("center", None),
            P("center"),
            P("center"),
            P(("center", "rep")),
        ),
        out_specs=(
            P(("center", "rep")),
            P(("center", "rep"), None),
            P("center", None),
            P("center", None),
        ),
        check_vma=False,
    )
```

time: 173 us -> 49.1 us (0.28)
  blocking collectives: 75.5 us -> 0 us
  waiting for transfers between devices: 56.7 us -> 18.4 us
  starting transfers between devices: 0.08 us -> 18.8 us
  between operations: 16.9 us -> 1.47 us
  Pallas kernels: 0 us -> 9.38 us
  other arithmetic: 8.98 us -> 0.05 us
  local copies, waits for them, and re-layouts: 8.84 us -> 0.68 us
  matrix products: 5.14 us -> 0 us
    reduce_scatter x1 -> x0, waiting for transfers between devices: 33 us -> none  [per_device(): lax.psum_scatter(unit_terms.reshape(group_rows, width), 'center', scatter...]
    all_gather x1 -> x0, blocking collectives: 31.2 us -> none  [per_device(): lax.all_gather(unit_low, 'center', axis=0, tiled=True)]
    psum x3 -> x0, blocking collectives: 31.2 us -> none  [the longest x1 18.9 us: per_device(): lax.psum((local_total.reshape(group_rows), local_target.reshape(group_row...]
    psum x1 -> x0, waiting for transfers between devices: 23.7 us -> none  [per_device(): raw_grad = lax.psum(center_raw, 'rep')]
    ppermute x0 -> x16, starting transfers between devices: none -> 18.8 us  [swap(): return lax.ppermute(value, axis, [(i, i ^ mask) for i in range(size)])]
    ppermute x0 -> x16, waiting for transfers between devices: none -> 18.4 us  [swap(): return lax.ppermute(value, axis, [(i, i ^ mask) for i in range(size)])]
    unnamed x1 -> x0, blocking collectives: 13.1 us -> none
    pallas_call x0 -> x11, Pallas kernels: none -> 9.38 us  [the longest x1 2.51 us: per_device(): pl.pallas_call(rows_kernel, in_specs=[HBM] * 3 + [VMEM], out_specs=[VMEM,...]
  transfers between devices with their start and end apart: 2 -> 16, of which waited for: 2 -> 10; matrix products, arithmetic and copies ran while one was open for 5% -> 0% of each run, Pallas kernels for 0% -> 12%
where the time goes in v1:
time: 49.1 us; the launch traced here: 48.8 us
  starting transfers between devices  18.8 us (38%)
  waiting for transfers between devices  18.4 us (37%)
  Pallas kernels  9.38 us (19%)
  between operations  1.47 us (3%)
  local copies, waits for them, and re-layouts  0.68 us (1%)
    ppermute x16, starting transfers between devices, swap(): return lax.ppermute(value, axis, [(i, i ^ mask) for i in range(size)])  18.8 us
    ppermute x16, waiting for transfers between devices, swap(): return lax.ppermute(value, axis, [(i, i ^ mask) for i in range(size)])  18.4 us
    pallas_call x1, Pallas kernels, per_device(): pl.pallas_call(rows_kernel, in_specs=[HBM] * 3 + [VMEM], out_specs=[VMEM,...  2.51 us
    pallas_call x1, Pallas kernels, per_device(): pl.pallas_call(head_kernel, in_specs=[HBM] * 2 + [VMEM] * 4, out_specs=[V...  2.17 us
    pallas_call x1, Pallas kernels, per_device(): pl.pallas_call(entry_kernel, in_specs=[HBM, SMEM, HBM, HBM, HBM], out_spe...  1.74 us
    pallas_call x1, Pallas kernels, per_device(): pl.pallas_call(functools.partial(step_kernel, masks), in_specs=[VMEM] * 4...  1.09 us
  transfers between devices with their start and end apart: 16, of which 10 were waited for; matrix products, arithmetic and copies ran while one was open for 0% of the time, Pallas kernels for 12%

profile of v1, /device:TPU:0, one launch (start us, length us, event | category | flops | bytes accessed | tf_op | source)
XLA Modules:
  0.0 48.8 jit_solution(14750653097805119675)
XLA Ops:
  1.3 1.7 %entry.1 = (bf16[32,512]{1,0:T(8,128)(2,1)S(1)}, bf16[80,512]{1,0:T(8,128)(2,1)S(1)}, s32[8,128]{1,0:T(8,128)S(1)}) custom-call(s32[128]{0:T(128)} %index_ref.3, s32[1]{0:T(128)S(6)} %copy.16.live_ref, f32[2048,512]{1,0:T(8,128)} %centers_ref.3, bf16[64,512]{1,0:T(8,128)(2,1)} %faces_ref.1, s32[1,64]{1,0:T(1,128)} %bitcast.9), custom_call_target="tpu_custom_call" | custom-call | tf_op jit(solution)/shard_map/entry/pallas_call | solution.py:262
  3.1 3.0 %collective-permute-start = (bf16[80,512]{1,0:T(8,128)(2,1)S(1)}, bf16[80,512]{1,0:T(8,128)(2,1)S(1)}, u32[]{:S(2)}, u32[]{:S(2)}) collective-permute-start(bf16[80,512]{1,0:T(8,128)(2,1)S(1)} %get-tuple-element.27), channel_id=1, source_target_pairs={{0,2},{1,3},{2,0},{3,1},{4,6},{5,7},{6,4},{7,5},{8,10},{9,11},{10,... | collective-permute-start | bytes 245768 | tf_op jit(solution)/shard_map/ppermute | solution.py:32
  6.1 1.5 %collective-permute-start.2 = (bf16[32,512]{1,0:T(8,128)(2,1)S(1)}, bf16[32,512]{1,0:T(8,128)(2,1)S(1)}, u32[]{:S(2)}, u32[]{:S(2)}) collective-permute-start(bf16[32,512]{1,0:T(8,128)(2,1)S(1)} %get-tuple-element.30), channel_id=1, source_target_pairs={{0,4},{4,0},{8,12},{12,8},{16,20},{20,16},{24,28},{28,24},{1,5},{5... | collective-permute-start | bytes 98312 | tf_op jit(solution)/shard_map/ppermute | solution.py:32
  7.6 0.9 %collective-permute-done = bf16[80,512]{1,0:T(8,128)(2,1)S(1)} collective-permute-done((bf16[80,512]{1,0:T(8,128)(2,1)S(1)}, bf16[80,512]{1,0:T(8,128)(2,1)S(1)}, u32[]{:S(2)}, u32[]{:S(2)}) %collective-permute-start) | collective-permute-done | bytes 81952 | tf_op jit(solution)/shard_map/ppermute | solution.py:32
  8.7 1.4 %collective-permute-done.2 = bf16[32,512]{1,0:T(8,128)(2,1)S(1)} collective-permute-done((bf16[32,512]{1,0:T(8,128)(2,1)S(1)}, bf16[32,512]{1,0:T(8,128)(2,1)S(1)}, u32[]{:S(2)}, u32[]{:S(2)}) %collective-permute-start.2) | collective-permute-done | bytes 32800 | tf_op jit(solution)/shard_map/ppermute | solution.py:32
  10.0 3.6 %collective-permute-start.5 = (bf16[64,512]{1,0:T(8,128)(2,1)S(1)}, bf16[64,512]{1,0:T(8,128)(2,1)S(1)}, u32[]{:S(2)}, u32[]{:S(2)}) collective-permute-start(bf16[64,512]{1,0:T(8,128)(2,1)S(1)} %constant_dynamic-update-slice_fusion.refs_0_), channel_id=1, source_target_pairs={{0,24},{4,28},{8,16},{12,20},{16,8},{20,12},{24,0},{28,4},{1,25},{... | collective-permute-start | bytes 196616 | tf_op jit(solution)/shard_map/ppermute | solution.py:32
  14.5 2.2 %head.1 = (bf16[256,512]{1,0:T(8,128)(2,1)S(1)}, f32[64,512]{1,0:T(8,128)S(1)}, s32[8,256]{1,0:T(8,128)S(1)}) custom-call(bf16[512,512]{1,0:T(8,128)(2,1)} %w_first_ref.1, bf16[512,512]{1,0:T(8,128)(2,1)} %w_second_ref.1, f32[1,512]{1,0:T(1,128)S(1)} %bitcast.5, f32[1,512]{1,0:T(1,128)S(1)} %bitcast.6, f32[1,512]{1,0:T(1,128)S(1)} %bitcast.7, ...), custom_call_target="tpu_custom_call" | custom-call | tf_op jit(solution)/shard_map/head/pallas_call | solution.py:292
  16.8 2.4 %collective-permute-done.4.refs_2_ = bf16[64,512]{1,0:T(8,128)(2,1)S(1)} collective-permute-done((bf16[64,512]{1,0:T(8,128)(2,1)S(1)}, bf16[64,512]{1,0:T(8,128)(2,1)S(1)}, u32[]{:S(2)}, u32[]{:S(2)}) %collective-permute-start.4) | collective-permute-done | bytes 65568 | tf_op jit(solution)/shard_map/ppermute | solution.py:32
  19.5 1.3 %collective-permute-start.6 = (f32[8,256]{1,0:T(8,128)S(1)}, f32[8,256]{1,0:T(8,128)S(1)}, u32[]{:S(2)}, u32[]{:S(2)}) collective-permute-start(f32[8,256]{1,0:T(8,128)S(1)} %get-tuple-element.32.own_ref), channel_id=1, source_target_pairs={{0,2},{1,3},{2,0},{3,1},{4,6},{5,7},{6,4},{7,5},{8,10},{9,11},{10,... | collective-permute-start | bytes 24584 | tf_op jit(solution)/shard_map/ppermute | solution.py:32
  20.8 2.4 %collective-permute-done.6.other_ref = f32[8,256]{1,0:T(8,128)S(1)} collective-permute-done((f32[8,256]{1,0:T(8,128)S(1)}, f32[8,256]{1,0:T(8,128)S(1)}, u32[]{:S(2)}, u32[]{:S(2)}) %collective-permute-start.6) | collective-permute-done | bytes 8224 | tf_op jit(solution)/shard_map/ppermute | solution.py:32
  23.2 1.2 %collective-permute-done.7.other_ref = f32[8,256]{1,0:T(8,128)S(1)} collective-permute-done((f32[8,256]{1,0:T(8,128)S(1)}, f32[8,256]{1,0:T(8,128)S(1)}, u32[]{:S(2)}, u32[]{:S(2)}) %collective-permute-start.7) | collective-permute-done | bytes 8224 | tf_op jit(solution)/shard_map/ppermute | solution.py:32
  25.0 1.5 %collective-permute-start.10 = (bf16[128,512]{1,0:T(8,128)(2,1)S(1)}, bf16[128,512]{1,0:T(8,128)(2,1)S(1)}, u32[]{:S(2)}, u32[]{:S(2)}) collective-permute-start(bf16[128,512]{1,0:T(8,128)(2,1)S(1)} %get-tuple-element.43), channel_id=1, source_target_pairs={{0,4},{4,0},{8,12},{12,8},{16,20},{20,16},{24,28},{28,24},{1,5},{5... | collective-permute-start | bytes 393224 | tf_op jit(solution)/shard_map/ppermute | solution.py:32
  26.6 1.2 %collective-permute-start.8 = (bf16[128,512]{1,0:T(8,128)(2,1)S(1)}, bf16[128,512]{1,0:T(8,128)(2,1)S(1)}, u32[]{:S(2)}, u32[]{:S(2)}) collective-permute-start(bf16[128,512]{1,0:T(8,128)(2,1)S(1)} %get-tuple-element.36), channel_id=1, source_target_pairs={{0,2},{1,3},{2,0},{3,1},{4,6},{5,7},{6,4},{7,5},{8,10},{9,11},{10,... | collective-permute-start | bytes 393224 | tf_op jit(solution)/shard_map/ppermute | solution.py:32
  27.8 2.8 %collective-permute-done.10.refs_0_ = bf16[128,512]{1,0:T(8,128)(2,1)S(1)} collective-permute-done((bf16[128,512]{1,0:T(8,128)(2,1)S(1)}, bf16[128,512]{1,0:T(8,128)(2,1)S(1)}, u32[]{:S(2)}, u32[]{:S(2)}) %collective-permute-start.10) | collective-permute-done | bytes 131104 | tf_op jit(solution)/shard_map/ppermute | solution.py:32
  30.7 1.0 %collective-permute-start.11 = (bf16[32,512]{1,0:T(8,128)(2,1)S(1)}, bf16[32,512]{1,0:T(8,128)(2,1)S(1)}, u32[]{:S(2)}, u32[]{:S(2)}) collective-permute-start(bf16[32,512]{1,0:T(8,128)(2,1)S(1)} %get-tuple-element.45), channel_id=1, source_target_pairs={{0,8},{4,12},{8,0},{12,4},{16,24},{20,28},{24,16},{28,20},{1,9},{5... | collective-permute-start | bytes 98312 | tf_op jit(solution)/shard_map/ppermute | solution.py:32
  31.7 2.2 %collective-permute-start.12 = (bf16[32,512]{1,0:T(8,128)(2,1)S(1)}, bf16[32,512]{1,0:T(8,128)(2,1)S(1)}, u32[]{:S(2)}, u32[]{:S(2)}) collective-permute-start(bf16[32,512]{1,0:T(8,128)(2,1)S(1)} %get-tuple-element.46), channel_id=1, source_target_pairs={{0,16},{4,20},{8,24},{12,28},{16,0},{20,4},{24,8},{28,12},{1,17},{... | collective-permute-start | bytes 98312 | tf_op jit(solution)/shard_map/ppermute | solution.py:32
  33.9 1.2 %collective-permute-start.13 = (bf16[32,512]{1,0:T(8,128)(2,1)S(1)}, bf16[32,512]{1,0:T(8,128)(2,1)S(1)}, u32[]{:S(2)}, u32[]{:S(2)}) collective-permute-start(bf16[32,512]{1,0:T(8,128)(2,1)S(1)} %get-tuple-element.47), channel_id=1, source_target_pairs={{0,24},{4,28},{8,16},{12,20},{16,8},{20,12},{24,0},{28,4},{1,25},{... | collective-permute-start | bytes 98312 | tf_op jit(solution)/shard_map/ppermute | solution.py:32
  35.1 1.4 %collective-permute-done.12.refs_1_ = bf16[32,512]{1,0:T(8,128)(2,1)S(1)} collective-permute-done((bf16[32,512]{1,0:T(8,128)(2,1)S(1)}, bf16[32,512]{1,0:T(8,128)(2,1)S(1)}, u32[]{:S(2)}, u32[]{:S(2)}) %collective-permute-start.12) | collective-permute-done | bytes 32800 | tf_op jit(solution)/shard_map/ppermute | solution.py:32
  36.5 3.1 %collective-permute-done.13.refs_2_ = bf16[32,512]{1,0:T(8,128)(2,1)S(1)} collective-permute-done((bf16[32,512]{1,0:T(8,128)(2,1)S(1)}, bf16[32,512]{1,0:T(8,128)(2,1)S(1)}, u32[]{:S(2)}, u32[]{:S(2)}) %collective-permute-start.13) | collective-permute-done | bytes 32800 | tf_op jit(solution)/shard_map/ppermute | solution.py:32
  39.6 1.2 %collective-permute-start.14 = (bf16[32,512]{1,0:T(8,128)(2,1)S(1)}, bf16[32,512]{1,0:T(8,128)(2,1)S(1)}, u32[]{:S(2)}, u32[]{:S(2)}) collective-permute-start(bf16[32,512]{1,0:T(8,128)(2,1)S(1)} %fold.3), channel_id=1, source_target_pairs={{0,2},{1,3},{2,0},{3,1},{4,6},{5,7},{6,4},{7,5},{8,10},{9,11},{10,... | collective-permute-start | bytes 98312 | tf_op jit(solution)/shard_map/ppermute | solution.py:32
  40.9 2.7 %collective-permute-done.14 = bf16[32,512]{1,0:T(8,128)(2,1)S(1)} collective-permute-done((bf16[32,512]{1,0:T(8,128)(2,1)S(1)}, bf16[32,512]{1,0:T(8,128)(2,1)S(1)}, u32[]{:S(2)}, u32[]{:S(2)}) %collective-permute-start.14) | collective-permute-done | bytes 32800 | tf_op jit(solution)/shard_map/ppermute | solution.py:32
  44.3 2.5 %rows.1 = (f32[128,512]{1,0:T(8,128)S(1)}, f32[128,512]{1,0:T(8,128)S(1)}) custom-call(s32[128]{0:T(128)} %index_ref.3, f32[2048,512]{1,0:T(8,128)} %centers_ref.3, f32[2048,512]{1,0:T(8,128)} %momentum_ref.1, f32[1,64]{1,0:T(1,128)S(1)} %copy-done.3), custom_call_target="tpu_custom_call" | custom-call | tf_op jit(solution)/shard_map/rows/pallas_call | solution.py:336
  46.8 0.9 %face.1 = f32[64,512]{1,0:T(8,128)} custom-call(f32[64,512]{1,0:T(8,128)S(1)} %get-tuple-element.34.feature_ref, f32[64,512]{1,0:T(8,128)S(1)} %get-tuple-element.37.own_ref, bf16[64,512]{1,0:T(8,128)(2,1)S(1)} %collective-permute-done.9.received_ref), custom_call_target="tpu_custom_call" | custom-call | tf_op jit(solution)/shard_map/face/pallas_call | solution.py:369
  47.7 1.1 %step.1 = (f32[128,512]{1,0:T(8,128)}, f32[128,512]{1,0:T(8,128)}) custom-call(s32[8,128]{1,0:T(8,128)S(1)} %get-tuple-element.39.live_ref, f32[128,512]{1,0:T(8,128)S(1)} %get-tuple-element.40.picked_ref, f32[128,512]{1,0:T(8,128)S(1)} %get-tuple-element.41.moment_ref, bf16[128,512]{1,0:T(8,128)(2,1)S(1)} %pad_maximum_fusion.2.raws_ref), custom_call_target="tpu_custom_call" | custom-call | tf_op jit(solution)/shard_map/step/pallas_call | solution.py:379
  (34 shorter events, 2.8 us)
Async XLA Ops:
  0.6 13.8 %copy-start.2 = (f32[512]{0:T(512)S(1)}, f32[512]{0:T(512)}, u32[]{:S(2)}) copy-start(f32[512]{0:T(512)} %param.16) | copy-start | bytes 6148
  0.6 13.8 %copy-start.1 = (f32[512]{0:T(512)S(1)}, f32[512]{0:T(512)}, u32[]{:S(2)}) copy-start(f32[512]{0:T(512)} %param.15) | copy-start | bytes 6148
  0.7 13.8 %copy-start = (f32[512]{0:T(512)S(1)}, f32[512]{0:T(512)}, u32[]{:S(2)}) copy-start(f32[512]{0:T(512)} %param.14) | copy-start | bytes 6148
  3.1 5.5 %collective-permute-start = (bf16[80,512]{1,0:T(8,128)(2,1)S(1)}, bf16[80,512]{1,0:T(8,128)(2,1)S(1)}, u32[]{:S(2)}, u32[]{:S(2)}) collective-permute-start(bf16[80,512]{1,0:T(8,128)(2,1)S(1)} %get-tuple-element.27), channel_id=1, source_target_pairs={{0,2},{1,3},{2,0},{3,1},{4,6},{5,7},{6,4},{7,5},{8,10},{9,11},{10,... | collective-permute-start | bytes 245768 | tf_op jit(solution)/shard_map/ppermute | solution.py:32
  6.1 3.9 %collective-permute-start.2 = (bf16[32,512]{1,0:T(8,128)(2,1)S(1)}, bf16[32,512]{1,0:T(8,128)(2,1)S(1)}, u32[]{:S(2)}, u32[]{:S(2)}) collective-permute-start(bf16[32,512]{1,0:T(8,128)(2,1)S(1)} %get-tuple-element.30), channel_id=1, source_target_pairs={{0,4},{4,0},{8,12},{12,8},{16,20},{20,16},{24,28},{28,24},{1,5},{5... | collective-permute-start | bytes 98312 | tf_op jit(solution)/shard_map/ppermute | solution.py:32
  8.6 5.9 %collective-permute-start.1 = (bf16[160,512]{1,0:T(8,128)(2,1)S(1)}, bf16[160,512]{1,0:T(8,128)(2,1)S(1)}, u32[]{:S(2)}, u32[]{:S(2)}) collective-permute-start(bf16[160,512]{1,0:T(8,128)(2,1)S(1)} %pad_maximum_fusion.1), channel_id=1, source_target_pairs={{0,1},{1,0},{2,3},{3,2},{4,5},{5,4},{6,7},{7,6},{8,9},{9,8},{10,11... | collective-permute-start | bytes 491528 | tf_op jit(solution)/shard_map/ppermute | solution.py:32
  10.0 6.7 %collective-permute-start.5 = (bf16[64,512]{1,0:T(8,128)(2,1)S(1)}, bf16[64,512]{1,0:T(8,128)(2,1)S(1)}, u32[]{:S(2)}, u32[]{:S(2)}) collective-permute-start(bf16[64,512]{1,0:T(8,128)(2,1)S(1)} %constant_dynamic-update-slice_fusion.refs_0_), channel_id=1, source_target_pairs={{0,24},{4,28},{8,16},{12,20},{16,8},{20,12},{24,0},{28,4},{1,25},{... | collective-permute-start | bytes 196616 | tf_op jit(solution)/shard_map/ppermute | solution.py:32
  13.6 5.6 %collective-permute-start.4 = (bf16[64,512]{1,0:T(8,128)(2,1)S(1)}, bf16[64,512]{1,0:T(8,128)(2,1)S(1)}, u32[]{:S(2)}, u32[]{:S(2)}) collective-permute-start(bf16[64,512]{1,0:T(8,128)(2,1)S(1)} %constant_dynamic-update-slice_fusion.refs_0_), channel_id=1, source_target_pairs={{0,16},{4,20},{8,24},{12,28},{16,0},{20,4},{24,8},{28,12},{1,17},{... | collective-permute-start | bytes 196616 | tf_op jit(solution)/shard_map/ppermute | solution.py:32
  13.6 5.6 %collective-permute-start.3 = (bf16[64,512]{1,0:T(8,128)(2,1)S(1)}, bf16[64,512]{1,0:T(8,128)(2,1)S(1)}, u32[]{:S(2)}, u32[]{:S(2)}) collective-permute-start(bf16[64,512]{1,0:T(8,128)(2,1)S(1)} %constant_dynamic-update-slice_fusion.refs_0_), channel_id=1, source_target_pairs={{0,8},{4,12},{8,0},{12,4},{16,24},{20,28},{24,16},{28,20},{1,9},{5... | collective-permute-start | bytes 196616 | tf_op jit(solution)/shard_map/ppermute | solution.py:32
  19.5 3.7 %collective-permute-start.6 = (f32[8,256]{1,0:T(8,128)S(1)}, f32[8,256]{1,0:T(8,128)S(1)}, u32[]{:S(2)}, u32[]{:S(2)}) collective-permute-start(f32[8,256]{1,0:T(8,128)S(1)} %get-tuple-element.32.own_ref), channel_id=1, source_target_pairs={{0,2},{1,3},{2,0},{3,1},{4,6},{5,7},{6,4},{7,5},{8,10},{9,11},{10,... | collective-permute-start | bytes 24584 | tf_op jit(solution)/shard_map/ppermute | solution.py:32
  23.2 1.2 %collective-permute-start.7 = (f32[8,256]{1,0:T(8,128)S(1)}, f32[8,256]{1,0:T(8,128)S(1)}, u32[]{:S(2)}, u32[]{:S(2)}) collective-permute-start(f32[8,256]{1,0:T(8,128)S(1)} %total.1.own_ref), channel_id=1, source_target_pairs={{0,1},{1,0},{2,3},{3,2},{4,5},{5,4},{6,7},{7,6},{8,9},{9,8},{10,11... | collective-permute-start | bytes 24584 | tf_op jit(solution)/shard_map/ppermute | solution.py:32
  25.0 5.6 %collective-permute-start.10 = (bf16[128,512]{1,0:T(8,128)(2,1)S(1)}, bf16[128,512]{1,0:T(8,128)(2,1)S(1)}, u32[]{:S(2)}, u32[]{:S(2)}) collective-permute-start(bf16[128,512]{1,0:T(8,128)(2,1)S(1)} %get-tuple-element.43), channel_id=1, source_target_pairs={{0,4},{4,0},{8,12},{12,8},{16,20},{20,16},{24,28},{28,24},{1,5},{5... | collective-permute-start | bytes 393224 | tf_op jit(solution)/shard_map/ppermute | solution.py:32
  26.6 14.2 %collective-permute-start.8 = (bf16[128,512]{1,0:T(8,128)(2,1)S(1)}, bf16[128,512]{1,0:T(8,128)(2,1)S(1)}, u32[]{:S(2)}, u32[]{:S(2)}) collective-permute-start(bf16[128,512]{1,0:T(8,128)(2,1)S(1)} %get-tuple-element.36), channel_id=1, source_target_pairs={{0,2},{1,3},{2,0},{3,1},{4,6},{5,7},{6,4},{7,5},{8,10},{9,11},{10,... | collective-permute-start | bytes 393224 | tf_op jit(solution)/shard_map/ppermute | solution.py:32
  30.7 4.5 %collective-permute-start.11 = (bf16[32,512]{1,0:T(8,128)(2,1)S(1)}, bf16[32,512]{1,0:T(8,128)(2,1)S(1)}, u32[]{:S(2)}, u32[]{:S(2)}) collective-permute-start(bf16[32,512]{1,0:T(8,128)(2,1)S(1)} %get-tuple-element.45), channel_id=1, source_target_pairs={{0,8},{4,12},{8,0},{12,4},{16,24},{20,28},{24,16},{28,20},{1,9},{5... | collective-permute-start | bytes 98312 | tf_op jit(solution)/shard_map/ppermute | solution.py:32
  31.7 4.8 %collective-permute-start.12 = (bf16[32,512]{1,0:T(8,128)(2,1)S(1)}, bf16[32,512]{1,0:T(8,128)(2,1)S(1)}, u32[]{:S(2)}, u32[]{:S(2)}) collective-permute-start(bf16[32,512]{1,0:T(8,128)(2,1)S(1)} %get-tuple-element.46), channel_id=1, source_target_pairs={{0,16},{4,20},{8,24},{12,28},{16,0},{20,4},{24,8},{28,12},{1,17},{... | collective-permute-start | bytes 98312 | tf_op jit(solution)/shard_map/ppermute | solution.py:32
  33.9 5.7 %collective-permute-start.13 = (bf16[32,512]{1,0:T(8,128)(2,1)S(1)}, bf16[32,512]{1,0:T(8,128)(2,1)S(1)}, u32[]{:S(2)}, u32[]{:S(2)}) collective-permute-start(bf16[32,512]{1,0:T(8,128)(2,1)S(1)} %get-tuple-element.47), channel_id=1, source_target_pairs={{0,24},{4,28},{8,16},{12,20},{16,8},{20,12},{24,0},{28,4},{1,25},{... | collective-permute-start | bytes 98312 | tf_op jit(solution)/shard_map/ppermute | solution.py:32
  39.6 4.0 %collective-permute-start.14 = (bf16[32,512]{1,0:T(8,128)(2,1)S(1)}, bf16[32,512]{1,0:T(8,128)(2,1)S(1)}, u32[]{:S(2)}, u32[]{:S(2)}) collective-permute-start(bf16[32,512]{1,0:T(8,128)(2,1)S(1)} %fold.3), channel_id=1, source_target_pairs={{0,2},{1,3},{2,0},{3,1},{4,6},{5,7},{6,4},{7,5},{8,10},{9,11},{10,... | collective-permute-start | bytes 98312 | tf_op jit(solution)/shard_map/ppermute | solution.py:32
  40.8 6.0 %collective-permute-start.9 = (bf16[64,512]{1,0:T(8,128)(2,1)S(1)}, bf16[64,512]{1,0:T(8,128)(2,1)S(1)}, u32[]{:S(2)}, u32[]{:S(2)}) collective-permute-start(bf16[64,512]{1,0:T(8,128)(2,1)S(1)} %get-tuple-element.38), channel_id=1, source_target_pairs={{0,1},{1,0},{2,3},{3,2},{4,5},{5,4},{6,7},{7,6},{8,9},{9,8},{10,11... | collective-permute-start | bytes 196616 | tf_op jit(solution)/shard_map/ppermute | solution.py:32
  43.6 4.1 %collective-permute-start.15 = (bf16[64,512]{1,0:T(8,128)(2,1)S(1)}, bf16[64,512]{1,0:T(8,128)(2,1)S(1)}, u32[]{:S(2)}, u32[]{:S(2)}) collective-permute-start(bf16[64,512]{1,0:T(8,128)(2,1)S(1)} %pad_maximum_fusion.3), channel_id=1, source_target_pairs={{0,1},{1,0},{2,3},{3,2},{4,5},{5,4},{6,7},{7,6},{8,9},{9,8},{10,11... | collective-permute-start | bytes 196616 | tf_op jit(solution)/shard_map/ppermute | solution.py:32
  43.6 0.7 %copy-start.3 = (f32[1,64]{1,0:T(1,128)S(1)}, f32[1,64]{1,0:T(1,128)}, u32[]{:S(2)}) copy-start(f32[1,64]{1,0:T(1,128)} %get-tuple-element.33.after_ref) | copy-start | bytes 772
